TPU v7x, 512 devices: a whole 4x8x8 slice. The times are simulated.
512 devices in a mesh: seq: 32 (over x, z), exp: 16 (over y, core).
Axes of the slice: x: 4, y: 8, z: 8, core: 2. Of those that a mesh axis runs over, the one named last changes fastest.
Arguments:
- queries: bfloat16 [8192, 2048], P('seq', 'exp'), may hold values from -112 to 112
- key_rows: bfloat16 [8192, 2048], P('seq', 'exp'), may hold values from -4 to 4
- value_rows: bfloat16 [8192, 2048], P('seq', 'exp'), may hold values from -6 to 6
- out_grad: bfloat16 [8192, 2048], P('seq', 'exp'), may hold values from -6 to 6
- expert_ids: int32 [8192, 2], P('seq'), may hold values from 0 to 31, all different within a row
- gate_values: float32 [8192, 2], P('seq'), may hold values from 0.1 to 1
- alibi_slope: float32 [16], P('exp'), may hold values from 0.00012207031 to 0.1
- expert_in: bfloat16 [32, 2048, 4096], P('seq', None, 'exp'), may hold values from -0.125 to 0.125
- expert_out: bfloat16 [32, 4096, 2048], P('seq', 'exp'), may hold values from -0.09375 to 0.09375
Outputs:
- query_grad: bfloat16 [8192, 2048], P('seq', 'exp')
- key_grad: bfloat16 [8192, 2048], P('seq', 'exp')
- value_grad: bfloat16 [8192, 2048], P('seq', 'exp')
- expert_in_grad: bfloat16 [32, 2048, 4096], P('seq', None, 'exp')
- expert_out_grad: bfloat16 [32, 4096, 2048], P('seq', 'exp')
Inputs may be any that keep to these rules, and one draw needn't show every extreme that they name: `expert_ids`: each token names two different experts.
All inputs are finite; a program needn't handle non-finite values.
Results may differ from a plain program's by a relative error of at most 0.024.
Values may be sent and summed in bfloat16 or wider, within the bound.
A program may use at most 128 MiB of HBM per device.

v0:
```python
import jax
import jax.numpy as jnp
from jax import lax
from jax.sharding import PartitionSpec as P

HD = 128
WCH = 16


def shifted(block, axis, distance):
    devices = range(lax.axis_size(axis))
    route = [(i - distance, i) for i in devices if i - distance in devices]
    return lax.ppermute(block, axis, route)


def window_scores(query_heads, key_stack, slopes, seq_index, window):
    score_scale = HD ** (-0.5)
    block_len = query_heads.shape[0]
    raw_scores = (
        jnp.einsum("ihd,jhd->hij", query_heads, key_stack, preferred_element_type=jnp.float32)
        * score_scale
    )
    row_pos = lax.broadcasted_iota(jnp.int32, (block_len, key_stack.shape[0]), 0)
    col_pos = lax.broadcasted_iota(jnp.int32, (block_len, key_stack.shape[0]), 1)
    back_block = col_pos // block_len
    distance = row_pos - col_pos % block_len + back_block * block_len
    in_window = (distance >= 0) & (distance < window) & (seq_index - back_block >= 0)
    biased = raw_scores - slopes[:, None, None] * distance.astype(jnp.float32)[None]
    return jnp.where(in_window[None], biased, -jnp.inf)


def slot_routing(expert_ids, experts, capacity):
    flat_ids = jnp.concatenate([expert_ids[:, 0], expert_ids[:, 1]])
    entry_count = flat_ids.shape[0]
    expert_cols = lax.broadcasted_iota(jnp.int32, (entry_count, experts), 1)
    one_hot = (flat_ids[:, None] == expert_cols).astype(jnp.int32)
    before = jnp.cumsum(one_hot, axis=0) - one_hot
    position = jnp.sum(before * one_hot, axis=1)
    is_kept = position < capacity
    slot_index = flat_ids * capacity + position
    slot_rows = lax.broadcasted_iota(jnp.int32, (experts * capacity, entry_count), 0)
    return ((slot_rows == slot_index[None, :]) & is_kept[None, :]).astype(jnp.bfloat16)


def per_device(
    queries,
    key_rows,
    value_rows,
    out_grad,
    expert_ids,
    gate_values,
    alibi_slope,
    expert_in,
    expert_out,
):
    score_scale = HD ** (-0.5)
    block_len = queries.shape[0]
    features = queries.shape[1]
    head_count = features // HD
    seq_index = lax.axis_index("seq")
    stretches = WCH + 1
    window = WCH * block_len

    def relay_keys(step, carry):
        stack_keys, stack_values, current_keys, current_values = carry
        current_keys, current_values = shifted((current_keys, current_values), "seq", 1)
        stack_keys = lax.dynamic_update_index_in_dim(stack_keys, current_keys, step, 0)
        stack_values = lax.dynamic_update_index_in_dim(stack_values, current_values, step, 0)
        return (stack_keys, stack_values, current_keys, current_values)

    empty_stack = jnp.zeros((stretches, block_len, features), jnp.bfloat16)
    start_keys = lax.dynamic_update_index_in_dim(empty_stack, key_rows, 0, 0)
    start_values = lax.dynamic_update_index_in_dim(empty_stack, value_rows, 0, 0)
    key_stack, value_stack, unused_keys, unused_values = lax.fori_loop(
        1, stretches, relay_keys, (start_keys, start_values, key_rows, value_rows)
    )
    key_block = key_stack.reshape(stretches * block_len, head_count, HD)
    value_block = value_stack.reshape(stretches * block_len, head_count, HD)
    query_heads = queries.reshape(block_len, head_count, HD)
    scores = window_scores(query_heads, key_block, alibi_slope, seq_index, window)
    log_norm = jax.nn.logsumexp(scores, axis=2)
    probs_full = jnp.exp(scores - log_norm[:, :, None])
    weights = probs_full.astype(jnp.bfloat16)
    attn_heads = jnp.einsum(
        "hij,jhd->ihd", weights, value_block, preferred_element_type=jnp.float32
    ).astype(jnp.bfloat16)
    attn_out = attn_heads.reshape(block_len, features)
    experts = lax.axis_size("seq")
    capacity = 5 * block_len // (2 * experts)
    routing = slot_routing(expert_ids, experts, capacity)
    both_tokens = jnp.concatenate([attn_out, attn_out])
    scaled_grad = jnp.concatenate(
        [gate_values[:, 0:1] * out_grad, gate_values[:, 1:2] * out_grad]
    ).astype(jnp.bfloat16)
    send_tokens = jnp.dot(routing, both_tokens, preferred_element_type=jnp.float32).astype(
        jnp.bfloat16
    )
    send_grads = jnp.dot(routing, scaled_grad, preferred_element_type=jnp.float32).astype(
        jnp.bfloat16
    )
    recv_tokens, recv_grads = (
        lax.all_to_all(send_tokens, "seq", split_axis=0, concat_axis=0, tiled=True),
        lax.all_to_all(send_grads, "seq", split_axis=0, concat_axis=0, tiled=True),
    )
    weight_in = expert_in[0]
    weight_out = expert_out[0]
    full_tokens = lax.all_gather(recv_tokens, "exp", axis=1, tiled=True)
    pre_act = jnp.dot(full_tokens, weight_in, preferred_element_type=jnp.float32)
    full_grads = lax.all_gather(recv_grads, "exp", axis=1, tiled=True)
    logistic = jax.nn.sigmoid(pre_act)
    hidden = (pre_act * logistic).astype(jnp.bfloat16)
    through_out = lax.dot_general(
        full_grads, weight_out, (((1,), (1,)), ((), ())), preferred_element_type=jnp.float32
    )
    hidden_grad = (through_out * logistic * (1.0 + pre_act * (1.0 - logistic))).astype(jnp.bfloat16)
    out_weight_grad = lax.dot_general(
        hidden, full_grads, (((0,), (0,)), ((), ())), preferred_element_type=jnp.float32
    ).astype(jnp.bfloat16)
    in_weight_grad = lax.dot_general(
        full_tokens, hidden_grad, (((0,), (0,)), ((), ())), preferred_element_type=jnp.float32
    ).astype(jnp.bfloat16)
    back_rows = lax.psum_scatter(
        lax.dot_general(
            weight_in, hidden_grad, (((1,), (1,)), ((), ())), preferred_element_type=jnp.float32
        ).astype(jnp.bfloat16),
        "exp",
        scatter_dimension=0,
        tiled=True,
    )
    returned = lax.all_to_all(back_rows, "seq", split_axis=1, concat_axis=1, tiled=True)
    combined = lax.dot_general(
        routing, returned, (((0,), (1,)), ((), ())), preferred_element_type=jnp.float32
    )
    attn_grad = (out_grad.astype(jnp.float32) + combined[:block_len] + combined[block_len:]).astype(
        jnp.bfloat16
    )
    grad_heads = attn_grad.reshape(block_len, head_count, HD)
    row_delta = jnp.einsum(
        "ihd,ihd->hi", grad_heads, attn_heads, preferred_element_type=jnp.float32
    )
    dprob = jnp.einsum("ihd,jhd->hij", grad_heads, value_block, preferred_element_type=jnp.float32)
    dscore = (probs_full * (dprob - row_delta[:, :, None])).astype(jnp.bfloat16)
    query_grad = (
        jnp.einsum("hij,jhd->ihd", dscore, key_block, preferred_element_type=jnp.float32)
        * score_scale
    ).astype(jnp.bfloat16)
    key_parts = (
        jnp.einsum("hij,ihd->jhd", dscore, query_heads, preferred_element_type=jnp.float32)
        * score_scale
    ).reshape(stretches, block_len, features)
    value_parts = jnp.einsum(
        "hij,ihd->jhd", weights, grad_heads, preferred_element_type=jnp.float32
    ).reshape(stretches, block_len, features)

    def relay_grads(step, carry):
        key_acc, value_acc = carry
        key_acc, value_acc = (
            shifted(key_acc.astype(jnp.bfloat16), "seq", -1).astype(key_acc.dtype),
            shifted(value_acc.astype(jnp.bfloat16), "seq", -1).astype(value_acc.dtype),
        )
        index = stretches - 1 - step
        key_acc = key_acc + lax.dynamic_index_in_dim(key_parts, index, 0, keepdims=False)
        value_acc = value_acc + lax.dynamic_index_in_dim(value_parts, index, 0, keepdims=False)
        return (key_acc, value_acc)

    key_total, value_total = lax.fori_loop(
        1, stretches, relay_grads, (key_parts[stretches - 1], value_parts[stretches - 1])
    )
    key_grad = key_total.astype(jnp.bfloat16)
    value_grad = value_total.astype(jnp.bfloat16)
    return (
        query_grad.reshape(block_len, features),
        key_grad,
        value_grad,
        in_weight_grad[None],
        out_weight_grad[None],
    )


def solution(mesh):
    return jax.shard_map(
        per_device,
        mesh=mesh,
        in_specs=(
            P("seq", "exp"),
            P("seq", "exp"),
            P("seq", "exp"),
            P("seq", "exp"),
            P("seq", None),
            P("seq", None),
            P("exp"),
            P("seq", None, "exp"),
            P("seq", "exp", None),
        ),
        out_specs=(
            P("seq", "exp"),
            P("seq", "exp"),
            P("seq", "exp"),
            P("seq", None, "exp"),
            P("seq", "exp", None),
        ),
        check_vma=False,
    )
```

profile of v0, /device:TPU:2, one launch (start us, length us, event | category | flops | bytes accessed | tf_op | source)
XLA Modules:
  0.0 586.6 jit_solution(2084339012505833438)
XLA Ops:
  14.8 170.1 %while.36 = (s32[]{:T(128)}, bf16[17,256,128]{2,1,0:T(8,128)(2,1)S(1)}, bf16[17,256,128]{2,1,0:T(8,128)(2,1)S(1)}, bf16[256,128]{1,0:T(8,128)(2,1)S(1)}, bf16[25...) while((s32[]{:T(128)}, bf16[17,256,128]{2,1,0:T(8,128)(2,1)S(1)}, ...), condition=%wide.region_1.2_spmd, body=%wide.region_0.1_spmd.sunk | while | flops 5 | bytes 1048783 | solution.py:74
  23.4 4.6 collective-permute-done.1
  85.1 4.4 collective-permute-done.1
  95.3 4.4 collective-permute-done.1
  106.2 5.0 collective-permute-done.1
  117.0 4.4 collective-permute-done.1
  127.3 5.0 collective-permute-done.1
  137.5 4.8 collective-permute-done.1
  147.8 4.4 collective-permute-done.1
  158.0 4.4 collective-permute-done.1
  168.3 4.4 collective-permute-done.1
  178.5 4.4 collective-permute-done.1
  184.9 5.8 fusion.71
  194.7 15.8 %all_to_all.36 = bf16[32,20,128]{2,1,0:T(8,128)(2,1)} all-to-all(bf16[32,20,128]{2,1,0:T(8,128)(2,1)S(1)} %all_to_all.27), channel_id=1, replica_groups=mesh['seq'=32,'exp'=16] {'seq'}, dimensions={0} | all-to-all | bytes 327680 | tf_op jit(solution)/shard_map/all_to_all | solution.py:102
  215.3 15.9 %all_to_all.37 = bf16[32,20,128]{2,1,0:T(8,128)(2,1)} all-to-all(bf16[32,20,128]{2,1,0:T(8,128)(2,1)S(1)} %all_to_all.24), channel_id=1, replica_groups=mesh['seq'=32,'exp'=16] {'seq'}, dimensions={0} | all-to-all | bytes 327680 | tf_op jit(solution)/shard_map/all_to_all | solution.py:103
  232.9 22.8 %all-gather.5.cloned.1.call-done = bf16[640,2048]{1,0:T(8,128)(2,1)} async-done(((bf16[640,128]{1,0:T(8,128)(2,1)}), bf16[640,2048]{1,0:T(8,128)(2,1)}) %all-gather.5.cloned.1.call-update) | async-done | bytes 2621456 | tf_op jit(solution)/shard_map/all_gather | solution.py:107
  259.2 43.8 %all-gather.3.cloned.1.call-done = bf16[640,2048]{1,0:T(8,128)(2,1)} async-done(((bf16[640,128]{1,0:T(8,128)(2,1)}), bf16[640,2048]{1,0:T(8,128)(2,1)}) %all-gather.3.cloned.1.call-update) | async-done | bytes 2621456 | tf_op jit(solution)/shard_map/all_gather | solution.py:109
  309.2 4.4 copy.33
  317.6 57.7 %reduce-scatter.4.cloned.1.call-done = bf16[128,640]{1,0:T(8,128)(2,1)} async-done(((bf16[2048,640]{1,0:T(8,128)(2,1)}), bf16[128,640]{1,0:T(8,128)(2,1)}) %reduce-scatter.4.cloned.1.call-update) | async-done | bytes 163856
  377.0 10.5 %all-to-all-start.2 = ((bf16[128,32,20]{0,2,1:T(8,128)(2,1)}), bf16[128,32,20]{0,2,1:T(8,128)(2,1)S(1)}, u32[]{:S(2)}, u32[]{:S(2)}) async-start(bf16[128,32,20]{0,2,1:T(8,128)(2,1)} %all_to_all.30), calls=%async_computation.2 | async-start | bytes 393216 | tf_op jit(solution)/shard_map/all_to_all | solution.py:130
  391.3 5.7 all-to-all-done.2
  412.9 166.5 %while.37 = (s32[]{:T(128)}, bf16[256,128]{1,0:T(8,128)(2,1)S(1)}, bf16[256,128]{1,0:T(8,128)(2,1)S(1)}, f32[17,256,128]{2,1,0:T(8,128)S(1)}, f32[17,256,128]{2,...) while((s32[]{:T(128)}, bf16[256,128]{1,0:T(8,128)(2,1)S(1)}, ...), condition=%wide.region_9.10_spmd, body=%wide.region_8.9_spmd.sunk | while | flops 196614 | bytes 1048803 | solution.py:166
  422.3 5.7 collective-permute-start.3
  537.3 4.6 collective-permute-start.3
  (288 shorter events, 327.6 us)
Async XLA Ops:
  7.2 248.6 %all-gather.5.cloned.1.call-start = ((), (), s32[]{:S(2)}) async-start(), calls=%async_computation.5 | async-start | bytes 2785280 | tf_op jit(solution)/shard_map/all_gather | solution.py:107
  14.8 13.2 %collective-permute-start.1 = (bf16[256,128]{1,0:T(8,128)(2,1)S(1)}, bf16[256,128]{1,0:T(8,128)(2,1)S(1)}, u32[]{:S(2)}, u32[]{:S(2)}) collective-permute-start(bf16[256,128]{1,0:T(8,128)(2,1)S(1)} %get-tuple-element.375), channel_id=1, source_target_pairs={{0,16},{16,32},{32,48},{48,64},{64,80},{80,96},{96,112},{112,128},... | collective-permute-start | bytes 196616 | tf_op jit(solution)/shard_map/while/body/eval_jaxpr/ppermute | solution.py:13
  19.1 10.8 %collective-permute-start = (bf16[256,128]{1,0:T(8,128)(2,1)S(1)}, bf16[256,128]{1,0:T(8,128)(2,1)S(1)}, u32[]{:S(2)}, u32[]{:S(2)}) collective-permute-start(bf16[256,128]{1,0:T(8,128)(2,1)S(1)} %get-tuple-element.374), channel_id=1, source_target_pairs={{0,16},{16,32},{32,48},{48,64},{64,80},{80,96},{96,112},{112,128},... | collective-permute-start | bytes 196616 | tf_op jit(solution)/shard_map/while/body/eval_jaxpr/ppermute | solution.py:13
  30.0 8.9 %collective-permute-start.1 = (bf16[256,128]{1,0:T(8,128)(2,1)S(1)}, bf16[256,128]{1,0:T(8,128)(2,1)S(1)}, u32[]{:S(2)}, u32[]{:S(2)}) collective-permute-start(bf16[256,128]{1,0:T(8,128)(2,1)S(1)} %get-tuple-element.375), channel_id=1, source_target_pairs={{0,16},{16,32},{32,48},{48,64},{64,80},{80,96},{96,112},{112,128},... | collective-permute-start | bytes 196616 | tf_op jit(solution)/shard_map/while/body/eval_jaxpr/ppermute | solution.py:13
  31.9 8.3 %collective-permute-start = (bf16[256,128]{1,0:T(8,128)(2,1)S(1)}, bf16[256,128]{1,0:T(8,128)(2,1)S(1)}, u32[]{:S(2)}, u32[]{:S(2)}) collective-permute-start(bf16[256,128]{1,0:T(8,128)(2,1)S(1)} %get-tuple-element.374), channel_id=1, source_target_pairs={{0,16},{16,32},{32,48},{48,64},{64,80},{80,96},{96,112},{112,128},... | collective-permute-start | bytes 196616 | tf_op jit(solution)/shard_map/while/body/eval_jaxpr/ppermute | solution.py:13
  40.2 8.7 %collective-permute-start.1 = (bf16[256,128]{1,0:T(8,128)(2,1)S(1)}, bf16[256,128]{1,0:T(8,128)(2,1)S(1)}, u32[]{:S(2)}, u32[]{:S(2)}) collective-permute-start(bf16[256,128]{1,0:T(8,128)(2,1)S(1)} %get-tuple-element.375), channel_id=1, source_target_pairs={{0,16},{16,32},{32,48},{48,64},{64,80},{80,96},{96,112},{112,128},... | collective-permute-start | bytes 196616 | tf_op jit(solution)/shard_map/while/body/eval_jaxpr/ppermute | solution.py:13
  42.1 8.3 %collective-permute-start = (bf16[256,128]{1,0:T(8,128)(2,1)S(1)}, bf16[256,128]{1,0:T(8,128)(2,1)S(1)}, u32[]{:S(2)}, u32[]{:S(2)}) collective-permute-start(bf16[256,128]{1,0:T(8,128)(2,1)S(1)} %get-tuple-element.374), channel_id=1, source_target_pairs={{0,16},{16,32},{32,48},{48,64},{64,80},{80,96},{96,112},{112,128},... | collective-permute-start | bytes 196616 | tf_op jit(solution)/shard_map/while/body/eval_jaxpr/ppermute | solution.py:13
  50.5 8.3 %collective-permute-start.1 = (bf16[256,128]{1,0:T(8,128)(2,1)S(1)}, bf16[256,128]{1,0:T(8,128)(2,1)S(1)}, u32[]{:S(2)}, u32[]{:S(2)}) collective-permute-start(bf16[256,128]{1,0:T(8,128)(2,1)S(1)} %get-tuple-element.375), channel_id=1, source_target_pairs={{0,16},{16,32},{32,48},{48,64},{64,80},{80,96},{96,112},{112,128},... | collective-permute-start | bytes 196616 | tf_op jit(solution)/shard_map/while/body/eval_jaxpr/ppermute | solution.py:13
  52.4 8.3 %collective-permute-start = (bf16[256,128]{1,0:T(8,128)(2,1)S(1)}, bf16[256,128]{1,0:T(8,128)(2,1)S(1)}, u32[]{:S(2)}, u32[]{:S(2)}) collective-permute-start(bf16[256,128]{1,0:T(8,128)(2,1)S(1)} %get-tuple-element.374), channel_id=1, source_target_pairs={{0,16},{16,32},{32,48},{48,64},{64,80},{80,96},{96,112},{112,128},... | collective-permute-start | bytes 196616 | tf_op jit(solution)/shard_map/while/body/eval_jaxpr/ppermute | solution.py:13
  60.7 8.3 %collective-permute-start.1 = (bf16[256,128]{1,0:T(8,128)(2,1)S(1)}, bf16[256,128]{1,0:T(8,128)(2,1)S(1)}, u32[]{:S(2)}, u32[]{:S(2)}) collective-permute-start(bf16[256,128]{1,0:T(8,128)(2,1)S(1)} %get-tuple-element.375), channel_id=1, source_target_pairs={{0,16},{16,32},{32,48},{48,64},{64,80},{80,96},{96,112},{112,128},... | collective-permute-start | bytes 196616 | tf_op jit(solution)/shard_map/while/body/eval_jaxpr/ppermute | solution.py:13
  62.6 8.3 %collective-permute-start = (bf16[256,128]{1,0:T(8,128)(2,1)S(1)}, bf16[256,128]{1,0:T(8,128)(2,1)S(1)}, u32[]{:S(2)}, u32[]{:S(2)}) collective-permute-start(bf16[256,128]{1,0:T(8,128)(2,1)S(1)} %get-tuple-element.374), channel_id=1, source_target_pairs={{0,16},{16,32},{32,48},{48,64},{64,80},{80,96},{96,112},{112,128},... | collective-permute-start | bytes 196616 | tf_op jit(solution)/shard_map/while/body/eval_jaxpr/ppermute | solution.py:13
  81.2 8.3 %collective-permute-start.1 = (bf16[256,128]{1,0:T(8,128)(2,1)S(1)}, bf16[256,128]{1,0:T(8,128)(2,1)S(1)}, u32[]{:S(2)}, u32[]{:S(2)}) collective-permute-start(bf16[256,128]{1,0:T(8,128)(2,1)S(1)} %get-tuple-element.375), channel_id=1, source_target_pairs={{0,16},{16,32},{32,48},{48,64},{64,80},{80,96},{96,112},{112,128},... | collective-permute-start | bytes 196616 | tf_op jit(solution)/shard_map/while/body/eval_jaxpr/ppermute | solution.py:13
  83.1 8.3 %collective-permute-start = (bf16[256,128]{1,0:T(8,128)(2,1)S(1)}, bf16[256,128]{1,0:T(8,128)(2,1)S(1)}, u32[]{:S(2)}, u32[]{:S(2)}) collective-permute-start(bf16[256,128]{1,0:T(8,128)(2,1)S(1)} %get-tuple-element.374), channel_id=1, source_target_pairs={{0,16},{16,32},{32,48},{48,64},{64,80},{80,96},{96,112},{112,128},... | collective-permute-start | bytes 196616 | tf_op jit(solution)/shard_map/while/body/eval_jaxpr/ppermute | solution.py:13
  93.4 8.9 %collective-permute-start = (bf16[256,128]{1,0:T(8,128)(2,1)S(1)}, bf16[256,128]{1,0:T(8,128)(2,1)S(1)}, u32[]{:S(2)}, u32[]{:S(2)}) collective-permute-start(bf16[256,128]{1,0:T(8,128)(2,1)S(1)} %get-tuple-element.374), channel_id=1, source_target_pairs={{0,16},{16,32},{32,48},{48,64},{64,80},{80,96},{96,112},{112,128},... | collective-permute-start | bytes 196616 | tf_op jit(solution)/shard_map/while/body/eval_jaxpr/ppermute | solution.py:13
  102.3 8.9 %collective-permute-start.1 = (bf16[256,128]{1,0:T(8,128)(2,1)S(1)}, bf16[256,128]{1,0:T(8,128)(2,1)S(1)}, u32[]{:S(2)}, u32[]{:S(2)}) collective-permute-start(bf16[256,128]{1,0:T(8,128)(2,1)S(1)} %get-tuple-element.375), channel_id=1, source_target_pairs={{0,16},{16,32},{32,48},{48,64},{64,80},{80,96},{96,112},{112,128},... | collective-permute-start | bytes 196616 | tf_op jit(solution)/shard_map/while/body/eval_jaxpr/ppermute | solution.py:13
  104.2 8.9 %collective-permute-start = (bf16[256,128]{1,0:T(8,128)(2,1)S(1)}, bf16[256,128]{1,0:T(8,128)(2,1)S(1)}, u32[]{:S(2)}, u32[]{:S(2)}) collective-permute-start(bf16[256,128]{1,0:T(8,128)(2,1)S(1)} %get-tuple-element.374), channel_id=1, source_target_pairs={{0,16},{16,32},{32,48},{48,64},{64,80},{80,96},{96,112},{112,128},... | collective-permute-start | bytes 196616 | tf_op jit(solution)/shard_map/while/body/eval_jaxpr/ppermute | solution.py:13
  123.4 8.9 %collective-permute-start.1 = (bf16[256,128]{1,0:T(8,128)(2,1)S(1)}, bf16[256,128]{1,0:T(8,128)(2,1)S(1)}, u32[]{:S(2)}, u32[]{:S(2)}) collective-permute-start(bf16[256,128]{1,0:T(8,128)(2,1)S(1)} %get-tuple-element.375), channel_id=1, source_target_pairs={{0,16},{16,32},{32,48},{48,64},{64,80},{80,96},{96,112},{112,128},... | collective-permute-start | bytes 196616 | tf_op jit(solution)/shard_map/while/body/eval_jaxpr/ppermute | solution.py:13
  133.7 8.7 %collective-permute-start.1 = (bf16[256,128]{1,0:T(8,128)(2,1)S(1)}, bf16[256,128]{1,0:T(8,128)(2,1)S(1)}, u32[]{:S(2)}, u32[]{:S(2)}) collective-permute-start(bf16[256,128]{1,0:T(8,128)(2,1)S(1)} %get-tuple-element.375), channel_id=1, source_target_pairs={{0,16},{16,32},{32,48},{48,64},{64,80},{80,96},{96,112},{112,128},... | collective-permute-start | bytes 196616 | tf_op jit(solution)/shard_map/while/body/eval_jaxpr/ppermute | solution.py:13
  135.6 8.3 %collective-permute-start = (bf16[256,128]{1,0:T(8,128)(2,1)S(1)}, bf16[256,128]{1,0:T(8,128)(2,1)S(1)}, u32[]{:S(2)}, u32[]{:S(2)}) collective-permute-start(bf16[256,128]{1,0:T(8,128)(2,1)S(1)} %get-tuple-element.374), channel_id=1, source_target_pairs={{0,16},{16,32},{32,48},{48,64},{64,80},{80,96},{96,112},{112,128},... | collective-permute-start | bytes 196616 | tf_op jit(solution)/shard_map/while/body/eval_jaxpr/ppermute | solution.py:13
  164.4 8.3 %collective-permute-start.1 = (bf16[256,128]{1,0:T(8,128)(2,1)S(1)}, bf16[256,128]{1,0:T(8,128)(2,1)S(1)}, u32[]{:S(2)}, u32[]{:S(2)}) collective-permute-start(bf16[256,128]{1,0:T(8,128)(2,1)S(1)} %get-tuple-element.375), channel_id=1, source_target_pairs={{0,16},{16,32},{32,48},{48,64},{64,80},{80,96},{96,112},{112,128},... | collective-permute-start | bytes 196616 | tf_op jit(solution)/shard_map/while/body/eval_jaxpr/ppermute | solution.py:13
  166.4 8.3 %collective-permute-start = (bf16[256,128]{1,0:T(8,128)(2,1)S(1)}, bf16[256,128]{1,0:T(8,128)(2,1)S(1)}, u32[]{:S(2)}, u32[]{:S(2)}) collective-permute-start(bf16[256,128]{1,0:T(8,128)(2,1)S(1)} %get-tuple-element.374), channel_id=1, source_target_pairs={{0,16},{16,32},{32,48},{48,64},{64,80},{80,96},{96,112},{112,128},... | collective-permute-start | bytes 196616 | tf_op jit(solution)/shard_map/while/body/eval_jaxpr/ppermute | solution.py:13
  212.2 90.8 %all-gather.3.cloned.1.call-start = ((), (), s32[]{:S(2)}) async-start(), calls=%async_computation.4 | async-start | bytes 2785280 | tf_op jit(solution)/shard_map/all_gather | solution.py:109
  232.9 142.4 %reduce-scatter.4.cloned.1.call-start = ((), (), s32[]{:S(2)}) async-start(), calls=%async_computation.6 | async-start | bytes 2785280
  377.0 20.0 %all-to-all-start.2 = ((bf16[128,32,20]{0,2,1:T(8,128)(2,1)}), bf16[128,32,20]{0,2,1:T(8,128)(2,1)S(1)}, u32[]{:S(2)}, u32[]{:S(2)}) async-start(bf16[128,32,20]{0,2,1:T(8,128)(2,1)} %all_to_all.30), calls=%async_computation.2 | async-start | bytes 393216 | tf_op jit(solution)/shard_map/all_to_all | solution.py:130
  (54 other events, 584.7 us)
Sparse Core Ops, SparseCore 0:
  212.3 43.3 all-gather.4
  258.4 44.5 all-gather.2
  313.7 61.4 reduce-scatter.3
where the time goes:
time: 590 us; the launch traced here: 587 us
  waiting for transfers between devices  277 us (47%)
  starting transfers between devices  183 us (31%)
  matrix products  35.4 us (6%)
  blocking collectives  31.8 us (5%)
  local copies, waits for them, and re-layouts  21.9 us (4%)
  other arithmetic  21.3 us (4%)
  between operations  14.7 us (2%)
    ppermute x64, starting transfers between devices, shifted(): return lax.ppermute(block, axis, route)  173 us
    ppermute x64, waiting for transfers between devices, shifted(): return lax.ppermute(block, axis, route)  147 us
    unnamed x4, waiting for transfers between devices  57.7 us
    all_gather x1, waiting for transfers between devices, per_device(): full_grads = lax.all_gather(recv_grads, 'exp', axis=1, tiled=True)  43.8 us
    all_gather x1, waiting for transfers between devices, per_device(): full_tokens = lax.all_gather(recv_tokens, 'exp', axis=1, tiled=True)  22.8 us
    all_to_all x1, blocking collectives, per_device(): lax.all_to_all(send_grads, 'seq', split_axis=0, concat_axis=0, tiled=True)  15.9 us
    all_to_all x1, blocking collectives, per_device(): lax.all_to_all(send_tokens, 'seq', split_axis=0, concat_axis=0, tiled=True)  15.8 us
    add x16, other arithmetic, relay_grads(): value_acc + lax.dynamic_index_in_dim(value_parts, index, 0, keepdims=False)  14.7 us
  transfers between devices with their start and end apart: 68, of which 64 were waited for; matrix products, arithmetic and copies ran while one was open for 5% of the time, Pallas kernels for 0%

commit v1 on v0

--- a/solution.py
+++ b/solution.py
@@ -104,7 +104,8 @@
     )
     weight_in = expert_in[0]
     weight_out = expert_out[0]
-    full_tokens = lax.all_gather(recv_tokens, "exp", axis=1, tiled=True)
+    copies = jnp.concatenate([recv_tokens] * lax.axis_size("exp"), axis=1)
+    full_tokens = lax.all_to_all(copies, "exp", 1, 1, tiled=True)
     pre_act = jnp.dot(full_tokens, weight_in, preferred_element_type=jnp.float32)
     full_grads = lax.all_gather(recv_grads, "exp", axis=1, tiled=True)
     logistic = jax.nn.sigmoid(pre_act)

time: 590 us -> 600 us (1.017)
  blocking collectives: 31.8 us -> 0 us
  starting transfers between devices: 183 us -> 203 us
  waiting for transfers between devices: 277 us -> 291 us
  local copies, waits for them, and re-layouts: 21.9 us -> 33.1 us
    all_to_all x0 -> x3, waiting for transfers between devices: none -> 83 us  [the longest x1 68.3 us: per_device(): full_tokens = lax.all_to_all(copies, 'exp', 1, 1, tiled=True)]
    all_gather x1, waiting for transfers between devices: 43.8 us -> 0.61 us  [per_device(): full_grads = lax.all_gather(recv_grads, 'exp', axis=1, tiled=True)]
    all_to_all x2 -> x0, blocking collectives: 31.8 us -> none  [the longest x1 15.9 us: per_device(): lax.all_to_all(send_grads, 'seq', split_axis=0, concat_axis=0, tiled=True)]
    all_gather x1 -> x0, waiting for transfers between devices: 22.8 us -> none  [per_device(): full_tokens = lax.all_gather(recv_tokens, 'exp', axis=1, tiled=True)]
    all_to_all x0 -> x3, starting transfers between devices: none -> 19.5 us  [the longest x1 7.25 us: per_device(): full_tokens = lax.all_to_all(copies, 'exp', 1, 1, tiled=True)]
    unnamed x4 -> x3, waiting for transfers between devices: 57.7 us -> 57.6 us
  transfers between devices with their start and end apart: 68 -> 70, of which waited for: 64 -> 67; matrix products, arithmetic and copies ran while one was open for 5% -> 5% of each run, Pallas kernels for 0% -> 0%
where the time goes in v1:
time: 600 us; the launch traced here: 597 us
  waiting for transfers between devices  291 us (48%)
  starting transfers between devices  203 us (34%)
  matrix products  33.8 us (6%)
  local copies, waits for them, and re-layouts  33.1 us (6%)
  other arithmetic  19.6 us (3%)
  between operations  15 us (2%)
    ppermute x64, starting transfers between devices, shifted(): return lax.ppermute(block, axis, route)  173 us
    ppermute x64, waiting for transfers between devices, shifted(): return lax.ppermute(block, axis, route)  147 us
    all_to_all x1, waiting for transfers between devices, per_device(): full_tokens = lax.all_to_all(copies, 'exp', 1, 1, tiled=True)  68.3 us
    unnamed x3, waiting for transfers between devices  57.6 us
    add x16, other arithmetic, relay_grads(): value_acc + lax.dynamic_index_in_dim(value_parts, index, 0, keepdims=False)  14.7 us
  transfers between devices with their start and end apart: 70, of which 67 were waited for; matrix products, arithmetic and copies ran while one was open for 5% of the time, Pallas kernels for 0%

profile of v1, /device:TPU:2, one launch (start us, length us, event | category | flops | bytes accessed | tf_op | source)
XLA Modules:
  0.0 597.1 jit_solution(14185082559193292566)
XLA Ops:
  14.8 170.1 %while.36 = (s32[]{:T(128)}, bf16[17,256,128]{2,1,0:T(8,128)(2,1)S(1)}, bf16[17,256,128]{2,1,0:T(8,128)(2,1)S(1)}, bf16[256,128]{1,0:T(8,128)(2,1)S(1)}, bf16[25...) while((s32[]{:T(128)}, bf16[17,256,128]{2,1,0:T(8,128)(2,1)S(1)}, ...), condition=%wide.region_1.2_spmd, body=%wide.region_0.1_spmd.sunk | while | flops 5 | bytes 1048783 | solution.py:74
  23.4 4.6 collective-permute-done.1
  85.1 4.4 collective-permute-done.1
  95.3 4.4 collective-permute-done.1
  106.1 5.0 collective-permute-done.1
  117.0 4.4 collective-permute-done.1
  127.3 5.0 collective-permute-done.1
  137.5 4.8 collective-permute-done.1
  147.8 4.4 collective-permute-done.1
  158.0 4.4 collective-permute-done.1
  168.3 4.4 collective-permute-done.1
  178.5 4.4 collective-permute-done.1
  184.9 5.8 fusion.71
  195.4 6.5 %all-to-all-start.1 = ((bf16[32,20,128]{2,1,0:T(8,128)(2,1)}), bf16[32,20,128]{2,1,0:T(8,128)(2,1)}, u32[]{:S(2)}, u32[]{:S(2)}) async-start(bf16[32,20,128]{2,1,0:T(8,128)(2,1)} %all_to_all.31), calls=%async_computation.1 | async-start | bytes 393216 | tf_op jit(solution)/shard_map/all_to_all | solution.py:102
  204.8 6.8 %all-to-all-done.1 = bf16[32,20,128]{2,1,0:T(8,128)(2,1)} async-done(((bf16[32,20,128]{2,1,0:T(8,128)(2,1)}), bf16[32,20,128]{2,1,0:T(8,128)(2,1)}, u32[]{:S(2)}, u32[]{:S(2)}) %all-to-all-start.1) | async-done | bytes 163872 | tf_op jit(solution)/shard_map/all_to_all | solution.py:102
  211.6 5.7 all-to-all-start
  218.9 7.9 %all-to-all-done = bf16[32,20,128]{2,1,0:T(8,128)(2,1)} async-done(((bf16[32,20,128]{2,1,0:T(8,128)(2,1)}), bf16[32,20,128]{2,1,0:T(8,128)(2,1)}, u32[]{:S(2)}, u32[]{:S(2)}) %all-to-all-start) | async-done | bytes 163872 | tf_op jit(solution)/shard_map/all_to_all | solution.py:103
  229.8 7.2 %all-to-all-start.2 = ((bf16[640,16,128]{2,0,1:T(8,128)(2,1)}), bf16[640,16,128]{2,0,1:T(8,128)(2,1)}, u32[]{:S(2)}, u32[]{:S(2)}) async-start(bf16[640,16,128]{2,0,1:T(8,128)(2,1)} %concatenate.40), calls=%async_computation.2 | async-start | bytes 5242880 | tf_op jit(solution)/shard_map/all_to_all | solution.py:108
  238.8 68.3 %all-to-all-done.2 = bf16[640,16,128]{2,0,1:T(8,128)(2,1)} async-done(((bf16[640,16,128]{2,0,1:T(8,128)(2,1)}), bf16[640,16,128]{2,0,1:T(8,128)(2,1)}, u32[]{:S(2)}, u32[]{:S(2)}) %all-to-all-start.2) | async-done | bytes 2621472 | tf_op jit(solution)/shard_map/all_to_all | solution.py:108
  326.2 57.6 %reduce-scatter.4.cloned.1.call-done = bf16[128,640]{1,0:T(8,128)(2,1)} async-done(((bf16[2048,640]{1,0:T(8,128)(2,1)}), bf16[128,640]{1,0:T(8,128)(2,1)}) %reduce-scatter.4.cloned.1.call-update) | async-done | bytes 163856
  387.1 10.6 %all-to-all-start.3 = ((bf16[128,32,20]{0,2,1:T(8,128)(2,1)}), bf16[128,32,20]{0,2,1:T(8,128)(2,1)}, u32[]{:S(2)}, u32[]{:S(2)}) async-start(bf16[128,32,20]{0,2,1:T(8,128)(2,1)} %all_to_all.35), calls=%async_computation.3 | async-start | bytes 393216 | tf_op jit(solution)/shard_map/all_to_all | solution.py:131
  423.2 166.5 %while.37 = (s32[]{:T(128)}, bf16[256,128]{1,0:T(8,128)(2,1)S(1)}, bf16[256,128]{1,0:T(8,128)(2,1)S(1)}, f32[17,256,128]{2,1,0:T(8,128)S(1)}, f32[17,256,128]{2,...) while((s32[]{:T(128)}, bf16[256,128]{1,0:T(8,128)(2,1)S(1)}, ...), condition=%wide.region_9.10_spmd, body=%wide.region_8.9_spmd.sunk | while | flops 196614 | bytes 1048803 | solution.py:167
  432.5 5.7 collective-permute-start.3
  547.5 4.6 collective-permute-start.3
  (297 shorter events, 343.9 us)
Async XLA Ops:
  14.8 13.2 %collective-permute-start.1 = (bf16[256,128]{1,0:T(8,128)(2,1)S(1)}, bf16[256,128]{1,0:T(8,128)(2,1)S(1)}, u32[]{:S(2)}, u32[]{:S(2)}) collective-permute-start(bf16[256,128]{1,0:T(8,128)(2,1)S(1)} %get-tuple-element.385), channel_id=1, source_target_pairs={{0,16},{16,32},{32,48},{48,64},{64,80},{80,96},{96,112},{112,128},... | collective-permute-start | bytes 196616 | tf_op jit(solution)/shard_map/while/body/eval_jaxpr/ppermute | solution.py:13
  19.1 10.8 %collective-permute-start = (bf16[256,128]{1,0:T(8,128)(2,1)S(1)}, bf16[256,128]{1,0:T(8,128)(2,1)S(1)}, u32[]{:S(2)}, u32[]{:S(2)}) collective-permute-start(bf16[256,128]{1,0:T(8,128)(2,1)S(1)} %get-tuple-element.384), channel_id=1, source_target_pairs={{0,16},{16,32},{32,48},{48,64},{64,80},{80,96},{96,112},{112,128},... | collective-permute-start | bytes 196616 | tf_op jit(solution)/shard_map/while/body/eval_jaxpr/ppermute | solution.py:13
  29.9 8.9 %collective-permute-start.1 = (bf16[256,128]{1,0:T(8,128)(2,1)S(1)}, bf16[256,128]{1,0:T(8,128)(2,1)S(1)}, u32[]{:S(2)}, u32[]{:S(2)}) collective-permute-start(bf16[256,128]{1,0:T(8,128)(2,1)S(1)} %get-tuple-element.385), channel_id=1, source_target_pairs={{0,16},{16,32},{32,48},{48,64},{64,80},{80,96},{96,112},{112,128},... | collective-permute-start | bytes 196616 | tf_op jit(solution)/shard_map/while/body/eval_jaxpr/ppermute | solution.py:13
  31.9 8.3 %collective-permute-start = (bf16[256,128]{1,0:T(8,128)(2,1)S(1)}, bf16[256,128]{1,0:T(8,128)(2,1)S(1)}, u32[]{:S(2)}, u32[]{:S(2)}) collective-permute-start(bf16[256,128]{1,0:T(8,128)(2,1)S(1)} %get-tuple-element.384), channel_id=1, source_target_pairs={{0,16},{16,32},{32,48},{48,64},{64,80},{80,96},{96,112},{112,128},... | collective-permute-start | bytes 196616 | tf_op jit(solution)/shard_map/while/body/eval_jaxpr/ppermute | solution.py:13
  40.2 8.7 %collective-permute-start.1 = (bf16[256,128]{1,0:T(8,128)(2,1)S(1)}, bf16[256,128]{1,0:T(8,128)(2,1)S(1)}, u32[]{:S(2)}, u32[]{:S(2)}) collective-permute-start(bf16[256,128]{1,0:T(8,128)(2,1)S(1)} %get-tuple-element.385), channel_id=1, source_target_pairs={{0,16},{16,32},{32,48},{48,64},{64,80},{80,96},{96,112},{112,128},... | collective-permute-start | bytes 196616 | tf_op jit(solution)/shard_map/while/body/eval_jaxpr/ppermute | solution.py:13
  50.4 8.3 %collective-permute-start.1 = (bf16[256,128]{1,0:T(8,128)(2,1)S(1)}, bf16[256,128]{1,0:T(8,128)(2,1)S(1)}, u32[]{:S(2)}, u32[]{:S(2)}) collective-permute-start(bf16[256,128]{1,0:T(8,128)(2,1)S(1)} %get-tuple-element.385), channel_id=1, source_target_pairs={{0,16},{16,32},{32,48},{48,64},{64,80},{80,96},{96,112},{112,128},... | collective-permute-start | bytes 196616 | tf_op jit(solution)/shard_map/while/body/eval_jaxpr/ppermute | solution.py:13
  62.6 8.3 %collective-permute-start = (bf16[256,128]{1,0:T(8,128)(2,1)S(1)}, bf16[256,128]{1,0:T(8,128)(2,1)S(1)}, u32[]{:S(2)}, u32[]{:S(2)}) collective-permute-start(bf16[256,128]{1,0:T(8,128)(2,1)S(1)} %get-tuple-element.384), channel_id=1, source_target_pairs={{0,16},{16,32},{32,48},{48,64},{64,80},{80,96},{96,112},{112,128},... | collective-permute-start | bytes 196616 | tf_op jit(solution)/shard_map/while/body/eval_jaxpr/ppermute | solution.py:13
  81.2 8.3 %collective-permute-start.1 = (bf16[256,128]{1,0:T(8,128)(2,1)S(1)}, bf16[256,128]{1,0:T(8,128)(2,1)S(1)}, u32[]{:S(2)}, u32[]{:S(2)}) collective-permute-start(bf16[256,128]{1,0:T(8,128)(2,1)S(1)} %get-tuple-element.385), channel_id=1, source_target_pairs={{0,16},{16,32},{32,48},{48,64},{64,80},{80,96},{96,112},{112,128},... | collective-permute-start | bytes 196616 | tf_op jit(solution)/shard_map/while/body/eval_jaxpr/ppermute | solution.py:13
  83.1 8.3 %collective-permute-start = (bf16[256,128]{1,0:T(8,128)(2,1)S(1)}, bf16[256,128]{1,0:T(8,128)(2,1)S(1)}, u32[]{:S(2)}, u32[]{:S(2)}) collective-permute-start(bf16[256,128]{1,0:T(8,128)(2,1)S(1)} %get-tuple-element.384), channel_id=1, source_target_pairs={{0,16},{16,32},{32,48},{48,64},{64,80},{80,96},{96,112},{112,128},... | collective-permute-start | bytes 196616 | tf_op jit(solution)/shard_map/while/body/eval_jaxpr/ppermute | solution.py:13
  93.4 8.9 %collective-permute-start = (bf16[256,128]{1,0:T(8,128)(2,1)S(1)}, bf16[256,128]{1,0:T(8,128)(2,1)S(1)}, u32[]{:S(2)}, u32[]{:S(2)}) collective-permute-start(bf16[256,128]{1,0:T(8,128)(2,1)S(1)} %get-tuple-element.384), channel_id=1, source_target_pairs={{0,16},{16,32},{32,48},{48,64},{64,80},{80,96},{96,112},{112,128},... | collective-permute-start | bytes 196616 | tf_op jit(solution)/shard_map/while/body/eval_jaxpr/ppermute | solution.py:13
  102.3 8.9 %collective-permute-start.1 = (bf16[256,128]{1,0:T(8,128)(2,1)S(1)}, bf16[256,128]{1,0:T(8,128)(2,1)S(1)}, u32[]{:S(2)}, u32[]{:S(2)}) collective-permute-start(bf16[256,128]{1,0:T(8,128)(2,1)S(1)} %get-tuple-element.385), channel_id=1, source_target_pairs={{0,16},{16,32},{32,48},{48,64},{64,80},{80,96},{96,112},{112,128},... | collective-permute-start | bytes 196616 | tf_op jit(solution)/shard_map/while/body/eval_jaxpr/ppermute | solution.py:13
  104.2 8.9 %collective-permute-start = (bf16[256,128]{1,0:T(8,128)(2,1)S(1)}, bf16[256,128]{1,0:T(8,128)(2,1)S(1)}, u32[]{:S(2)}, u32[]{:S(2)}) collective-permute-start(bf16[256,128]{1,0:T(8,128)(2,1)S(1)} %get-tuple-element.384), channel_id=1, source_target_pairs={{0,16},{16,32},{32,48},{48,64},{64,80},{80,96},{96,112},{112,128},... | collective-permute-start | bytes 196616 | tf_op jit(solution)/shard_map/while/body/eval_jaxpr/ppermute | solution.py:13
  113.1 8.3 %collective-permute-start.1 = (bf16[256,128]{1,0:T(8,128)(2,1)S(1)}, bf16[256,128]{1,0:T(8,128)(2,1)S(1)}, u32[]{:S(2)}, u32[]{:S(2)}) collective-permute-start(bf16[256,128]{1,0:T(8,128)(2,1)S(1)} %get-tuple-element.385), channel_id=1, source_target_pairs={{0,16},{16,32},{32,48},{48,64},{64,80},{80,96},{96,112},{112,128},... | collective-permute-start | bytes 196616 | tf_op jit(solution)/shard_map/while/body/eval_jaxpr/ppermute | solution.py:13
  115.1 8.3 %collective-permute-start = (bf16[256,128]{1,0:T(8,128)(2,1)S(1)}, bf16[256,128]{1,0:T(8,128)(2,1)S(1)}, u32[]{:S(2)}, u32[]{:S(2)}) collective-permute-start(bf16[256,128]{1,0:T(8,128)(2,1)S(1)} %get-tuple-element.384), channel_id=1, source_target_pairs={{0,16},{16,32},{32,48},{48,64},{64,80},{80,96},{96,112},{112,128},... | collective-permute-start | bytes 196616 | tf_op jit(solution)/shard_map/while/body/eval_jaxpr/ppermute | solution.py:13
  123.4 8.9 %collective-permute-start.1 = (bf16[256,128]{1,0:T(8,128)(2,1)S(1)}, bf16[256,128]{1,0:T(8,128)(2,1)S(1)}, u32[]{:S(2)}, u32[]{:S(2)}) collective-permute-start(bf16[256,128]{1,0:T(8,128)(2,1)S(1)} %get-tuple-element.385), channel_id=1, source_target_pairs={{0,16},{16,32},{32,48},{48,64},{64,80},{80,96},{96,112},{112,128},... | collective-permute-start | bytes 196616 | tf_op jit(solution)/shard_map/while/body/eval_jaxpr/ppermute | solution.py:13
  133.7 8.7 %collective-permute-start.1 = (bf16[256,128]{1,0:T(8,128)(2,1)S(1)}, bf16[256,128]{1,0:T(8,128)(2,1)S(1)}, u32[]{:S(2)}, u32[]{:S(2)}) collective-permute-start(bf16[256,128]{1,0:T(8,128)(2,1)S(1)} %get-tuple-element.385), channel_id=1, source_target_pairs={{0,16},{16,32},{32,48},{48,64},{64,80},{80,96},{96,112},{112,128},... | collective-permute-start | bytes 196616 | tf_op jit(solution)/shard_map/while/body/eval_jaxpr/ppermute | solution.py:13
  135.6 8.3 %collective-permute-start = (bf16[256,128]{1,0:T(8,128)(2,1)S(1)}, bf16[256,128]{1,0:T(8,128)(2,1)S(1)}, u32[]{:S(2)}, u32[]{:S(2)}) collective-permute-start(bf16[256,128]{1,0:T(8,128)(2,1)S(1)} %get-tuple-element.384), channel_id=1, source_target_pairs={{0,16},{16,32},{32,48},{48,64},{64,80},{80,96},{96,112},{112,128},... | collective-permute-start | bytes 196616 | tf_op jit(solution)/shard_map/while/body/eval_jaxpr/ppermute | solution.py:13
  164.4 8.3 %collective-permute-start.1 = (bf16[256,128]{1,0:T(8,128)(2,1)S(1)}, bf16[256,128]{1,0:T(8,128)(2,1)S(1)}, u32[]{:S(2)}, u32[]{:S(2)}) collective-permute-start(bf16[256,128]{1,0:T(8,128)(2,1)S(1)} %get-tuple-element.385), channel_id=1, source_target_pairs={{0,16},{16,32},{32,48},{48,64},{64,80},{80,96},{96,112},{112,128},... | collective-permute-start | bytes 196616 | tf_op jit(solution)/shard_map/while/body/eval_jaxpr/ppermute | solution.py:13
  195.4 16.2 %all-to-all-start.1 = ((bf16[32,20,128]{2,1,0:T(8,128)(2,1)}), bf16[32,20,128]{2,1,0:T(8,128)(2,1)}, u32[]{:S(2)}, u32[]{:S(2)}) async-start(bf16[32,20,128]{2,1,0:T(8,128)(2,1)} %all_to_all.31), calls=%async_computation.1 | async-start | bytes 393216 | tf_op jit(solution)/shard_map/all_to_all | solution.py:102
  211.6 15.2 %all-to-all-start = ((bf16[32,20,128]{2,1,0:T(8,128)(2,1)}), bf16[32,20,128]{2,1,0:T(8,128)(2,1)}, u32[]{:S(2)}, u32[]{:S(2)}) async-start(bf16[32,20,128]{2,1,0:T(8,128)(2,1)} %all_to_all.28), calls=%async_computation | async-start | bytes 393216 | tf_op jit(solution)/shard_map/all_to_all | solution.py:103
  229.8 77.3 %all-to-all-start.2 = ((bf16[640,16,128]{2,0,1:T(8,128)(2,1)}), bf16[640,16,128]{2,0,1:T(8,128)(2,1)}, u32[]{:S(2)}, u32[]{:S(2)}) async-start(bf16[640,16,128]{2,0,1:T(8,128)(2,1)} %concatenate.40), calls=%async_computation.2 | async-start | bytes 5242880 | tf_op jit(solution)/shard_map/all_to_all | solution.py:108
  237.0 78.5 %all-gather.2.cloned.1.call-start = ((), (), s32[]{:S(2)}) async-start(), calls=%async_computation.5 | async-start | bytes 2785280 | tf_op jit(solution)/shard_map/all_gather | solution.py:110
  238.7 145.0 %reduce-scatter.4.cloned.1.call-start = ((), (), s32[]{:S(2)}) async-start(), calls=%async_computation.6 | async-start | bytes 2785280
  387.1 20.1 %all-to-all-start.3 = ((bf16[128,32,20]{0,2,1:T(8,128)(2,1)}), bf16[128,32,20]{0,2,1:T(8,128)(2,1)}, u32[]{:S(2)}, u32[]{:S(2)}) async-start(bf16[128,32,20]{0,2,1:T(8,128)(2,1)} %all_to_all.35), calls=%async_computation.3 | async-start | bytes 393216 | tf_op jit(solution)/shard_map/all_to_all | solution.py:131
  (59 other events, 665.6 us)
Sparse Core Ops, SparseCore 0:
  240.5 75.0 all-gather.1
  326.3 57.4 reduce-scatter.3
